TPU v7x, 512 devices: a whole 4x8x8 slice. The times are simulated.
512 devices in a mesh: round: 128 (over z, y, core), mp: 4 (over x).
Axes of the slice: x: 4, y: 8, z: 8, core: 2. Of those that a mesh axis runs over, the one named last changes fastest.
Arguments:
- tokens: bfloat16 [128, 512, 512], P('round'), may hold values from -8 to 8
- cell_order: int32 [512], replicated, may hold values from 0 to 511, each once
- seam_rows: int32 [128, 128, 2], P('round'), may hold values from -1 to 511, as said below
- obs_mask: int32 [16, 512], replicated, may hold values from 0 to 1, as said below
- norm_gain: float32 [512], replicated, may hold values from 0.1 to 1.9
- w_query: bfloat16 [512, 512], P(None, 'mp'), may hold values from -1 to 1
- w_key: bfloat16 [512, 512], P(None, 'mp'), may hold values from -1 to 1
- w_value: bfloat16 [512, 512], P(None, 'mp'), may hold values from -0.25 to 0.25
- w_out: bfloat16 [512, 512], P('mp'), may hold values from -0.25 to 0.25
- w_gate: bfloat16 [512, 2048], P(None, 'mp'), may hold values from -0.25 to 0.25
- w_up: bfloat16 [512, 2048], P(None, 'mp'), may hold values from -0.25 to 0.25
- w_down: bfloat16 [2048, 512], P('mp'), may hold values from -0.125 to 0.125
- w_read: float32 [512], replicated, may hold values from -0.25 to 0.25
Outputs:
- tiles_out: bfloat16 [128, 512, 512], P('mp', 'round')
- obs_logits: float32 [16], replicated
Inputs may be any that keep to these rules, and one draw needn't show every extreme that they name: `seam_rows`: each entry is a row of the sending tile or -1 for an empty slot; the live entries of one tile are all different; a tile's slots to itself are full, and some owner's slots are full from every tile. `obs_mask`: every observable's support holds at least one cell.
All inputs are finite; a program needn't handle non-finite values.
Results may differ from a plain program's by a relative error of at most 0.0052.
The roundings to bfloat16 on the way count: a program that leaves them out, or rounds other values in their place, can miss the bound.
Values may be sent and summed in bfloat16 or wider, within the bound.
A program may use at most 64 MiB of HBM per device.

v0:
```python
import math
import jax
import jax.numpy as jnp
from jax import lax
from jax.sharding import PartitionSpec as P

HDIM = 64
norm_eps = 1e-06


def normalize(rows_in, norm_gain):
    values = rows_in.astype(jnp.float32)
    spread = jnp.mean(values * values, axis=-1, keepdims=True)
    return (values * lax.rsqrt(spread + norm_eps) * norm_gain).astype(jnp.bfloat16)


def attend(queries, keys_all, values_all, live_keys):
    scale_factor = 1.0 / math.sqrt(queries.shape[-1])
    scores = (
        jnp.einsum("qhe,khe->hqk", queries, keys_all, preferred_element_type=jnp.float32)
        * scale_factor
    )
    if live_keys is not None:
        scores = jnp.where(live_keys[None, None, :], scores, -1e30)
    row_max = jnp.max(scores, axis=-1, keepdims=True)
    weights = jnp.exp(scores - row_max)
    probabilities = (weights / jnp.sum(weights, axis=-1, keepdims=True)).astype(jnp.bfloat16)
    mixture = jnp.einsum(
        "hqk,khe->qhe", probabilities, values_all, preferred_element_type=jnp.float32
    )
    return mixture.reshape(mixture.shape[0], -1)


def shards(
    tokens,
    cell_order,
    seam_rows,
    obs_mask,
    norm_gain,
    w_query,
    w_key,
    w_value,
    w_out,
    w_gate,
    w_up,
    w_down,
    w_read,
):
    round_count = lax.axis_size("round")
    model_count = lax.axis_size("mp")
    model_index = lax.axis_index("mp")
    round_index = lax.axis_index("round")
    width = tokens.shape[2]
    cell_dev = tokens.shape[1] // round_count
    permuted = tokens[:, cell_order, :]
    tile_tokens = lax.all_to_all(permuted, "round", split_axis=1, concat_axis=0, tiled=True)
    tile_rows = tile_tokens.shape[0] * cell_dev
    flat_tokens = tile_tokens.reshape(tile_rows, width)
    normed = normalize(flat_tokens, norm_gain)
    queries = jnp.dot(normed, w_query, preferred_element_type=jnp.float32).astype(jnp.bfloat16)
    keys_all = jnp.dot(normed, w_key, preferred_element_type=jnp.float32).astype(jnp.bfloat16)
    values_all = jnp.dot(normed, w_value, preferred_element_type=jnp.float32).astype(jnp.bfloat16)
    head_width = queries.shape[1]
    heads_dev = head_width // HDIM
    block_rows = min(512, tile_rows)
    query_blocks = queries.reshape(tile_rows // block_rows, block_rows, heads_dev, HDIM)
    key_heads = keys_all.reshape(tile_rows, heads_dev, HDIM)
    value_heads = values_all.reshape(tile_rows, heads_dev, HDIM)
    local_attn = lax.map(
        lambda query_block: attend(query_block, key_heads, value_heads, None), query_blocks
    )
    local_attn = local_attn.reshape(tile_rows, head_width)
    live_slot = seam_rows[0] >= 0
    safe_rows = jnp.where(live_slot, seam_rows[0], 0)
    packet = (
        lax.all_to_all(queries[safe_rows], "round", split_axis=0, concat_axis=0, tiled=True),
        lax.all_to_all(keys_all[safe_rows], "round", split_axis=0, concat_axis=0, tiled=True),
        lax.all_to_all(values_all[safe_rows], "round", split_axis=0, concat_axis=0, tiled=True),
        lax.all_to_all(
            live_slot.astype(jnp.bfloat16), "round", split_axis=0, concat_axis=0, tiled=True
        ),
    )
    seam_queries = packet[0].reshape(-1, heads_dev, HDIM)
    seam_keys = packet[1].reshape(-1, heads_dev, HDIM)
    seam_values = packet[2].reshape(-1, heads_dev, HDIM)
    seam_live = packet[3].reshape(-1) > 0.5
    seam_attn = attend(seam_queries, seam_keys, seam_values, seam_live).astype(jnp.bfloat16)
    returned = lax.all_to_all(
        seam_attn.reshape(round_count, -1, head_width),
        "round",
        split_axis=0,
        concat_axis=0,
        tiled=True,
    )
    target = jnp.where(live_slot, seam_rows[0], tile_rows).reshape(-1)
    combined = (
        local_attn.at[target]
        .add(returned.reshape(-1, head_width).astype(jnp.float32), mode="drop")
        .astype(jnp.bfloat16)
    )
    share_rows = tile_rows // model_count
    own_first = model_index * share_rows
    gate_part = jnp.dot(normed, w_gate, preferred_element_type=jnp.float32)
    up_part = jnp.dot(normed, w_up, preferred_element_type=jnp.float32)
    hidden = (jax.nn.silu(gate_part) * up_part).astype(jnp.bfloat16)
    attn_part = jnp.dot(combined, w_out, preferred_element_type=jnp.float32)
    summed = lax.psum_scatter(
        attn_part + jnp.dot(hidden, w_down, preferred_element_type=jnp.float32),
        "mp",
        scatter_dimension=0,
        tiled=True,
    )
    own_rows = lax.dynamic_slice_in_dim(flat_tokens, own_first, share_rows, 0)
    result_rows = (own_rows.astype(jnp.float32) + summed).astype(jnp.bfloat16)
    tiles_out = result_rows.reshape(share_rows // cell_dev, cell_dev, width)
    my_cells = lax.dynamic_slice_in_dim(cell_order, round_index * cell_dev, cell_dev)
    support = obs_mask[:, my_cells].astype(jnp.float32)
    partial_sum = jnp.einsum(
        "oc,rcd->od", support, tiles_out.astype(jnp.float32), precision=lax.Precision.HIGHEST
    )
    support_count = round_count * jnp.sum(obs_mask.astype(jnp.float32), axis=1)
    divisor = jnp.sqrt(support_count)
    pooled = lax.psum(partial_sum, ("round", "mp"))
    obs_logits = jnp.dot(pooled, w_read, precision=lax.Precision.HIGHEST) / divisor
    return (tiles_out, obs_logits)


def solution(mesh):
    return jax.shard_map(
        shards,
        mesh=mesh,
        in_specs=(
            P("round", None, None),
            P(),
            P("round", None, None),
            P(),
            P(),
            P(None, "mp"),
            P(None, "mp"),
            P(None, "mp"),
            P("mp", None),
            P(None, "mp"),
            P(None, "mp"),
            P("mp", None),
            P(),
        ),
        out_specs=(P("mp", "round", None), P()),
        check_vma=False,
    )
```

profile of v0, /device:TPU:1, one launch (start us, length us, event | category | flops | bytes accessed | tf_op | source)
XLA Modules:
  0.0 291.0 jit_solution(16656046799085090074)
XLA Ops:
  8.7 18.4 %all-to-all-start.2 = ((bf16[128,1,2]{2,1,0:T(2,128)(2,1)}), bf16[128,1,2]{2,1,0:T(2,128)(2,1)S(1)}, u32[]{:S(2)}, u32[]{:S(2)}) async-start(bf16[128,1,2]{2,1,0:T(2,128)(2,1)} %copy.61), calls=%async_computation.2 | async-start | bytes 131072 | tf_op jit(solution)/shard_map/all_to_all | solution.py:79
  27.8 2.0 gather_fusion
  31.1 3.8 %reduce.2 = bf16[512,512]{1,0:T(8,128)(2,1)S(1)} reduce(bf16[512,1,512]{2,1,0:T(2,128)(2,1)S(1)} %bitcast.69, bf16[]{:T(256)} %broadcast.153), dimensions={1}, to_apply=%bitcast.66.reduce_sub_computation | reduce | bytes 1048578
  35.0 1.1 reshape.218
  36.1 2.4 all-to-all-done.2
  38.5 11.3 %all-to-all-start = ((bf16[128,2,1024]{2,1,0:T(2,128)(2,1)}), bf16[128,2,1024]{2,1,0:T(2,128)(2,1)S(1)}, u32[]{:S(2)}, u32[]{:S(2)}) async-start(bf16[128,2,1024]{2,1,0:T(2,128)(2,1)} %reshape.218), calls=%async_computation | async-start | bytes 1048576 | tf_op jit(solution)/shard_map/all_to_all | solution.py:56
  50.8 19.6 %all-to-all-done = bf16[128,2,1024]{2,1,0:T(2,128)(2,1)S(1)} async-done(((bf16[128,2,1024]{2,1,0:T(2,128)(2,1)}), bf16[128,2,1024]{2,1,0:T(2,128)(2,1)S(1)}, u32[]{:S(2)}, u32[]{:S(2)}) %all-to-all-start) | async-done | bytes 524320 | tf_op jit(solution)/shard_map/all_to_all | solution.py:56
  70.9 1.1 bitcast_convert_fusion
  74.1 1.5 gather_fusion.1
  75.6 1.5 gather_fusion.2
  77.0 6.3 %all-to-all-start.3 = ((bf16[128,2,128]{2,1,0:T(2,128)(2,1)}), bf16[128,2,128]{2,1,0:T(2,128)(2,1)}, u32[]{:S(2)}, u32[]{:S(2)}) async-start(bf16[128,2,128]{2,1,0:T(2,128)(2,1)} %bitcast.12), calls=%async_computation.3 | async-start | bytes 131072 | tf_op jit(solution)/shard_map/all_to_all | solution.py:76
  83.3 1.5 fusion.55
  86.8 1.5 gather_fusion.3
  88.3 5.8 %all-to-all-done.3 = bf16[128,2,128]{2,1,0:T(2,128)(2,1)} async-done(((bf16[128,2,128]{2,1,0:T(2,128)(2,1)}), bf16[128,2,128]{2,1,0:T(2,128)(2,1)}, u32[]{:S(2)}, u32[]{:S(2)}) %all-to-all-start.3) | async-done | bytes 65568 | tf_op jit(solution)/shard_map/all_to_all | solution.py:76
  94.1 8.0 %all-to-all-start.4 = ((bf16[128,2,128]{2,1,0:T(2,128)(2,1)}), bf16[128,2,128]{2,1,0:T(2,128)(2,1)}, u32[]{:S(2)}, u32[]{:S(2)}) async-start(bf16[128,2,128]{2,1,0:T(2,128)(2,1)} %bitcast.78), calls=%async_computation.4 | async-start | bytes 131072 | tf_op jit(solution)/shard_map/all_to_all | solution.py:77
  102.1 1.7 fusion.49
  104.8 8.5 %all-to-all-done.4 = bf16[128,2,128]{2,1,0:T(2,128)(2,1)} async-done(((bf16[128,2,128]{2,1,0:T(2,128)(2,1)}), bf16[128,2,128]{2,1,0:T(2,128)(2,1)}, u32[]{:S(2)}, u32[]{:S(2)}) %all-to-all-start.4) | async-done | bytes 65568 | tf_op jit(solution)/shard_map/all_to_all | solution.py:77
  113.3 6.9 %all-to-all-start.1 = ((bf16[128,2,128]{2,1,0:T(2,128)(2,1)}), bf16[128,2,128]{2,1,0:T(2,128)(2,1)}, u32[]{:S(2)}, u32[]{:S(2)}) async-start(bf16[128,2,128]{2,1,0:T(2,128)(2,1)} %bitcast.76), calls=%async_computation.1 | async-start | bytes 131072 | tf_op jit(solution)/shard_map/all_to_all | solution.py:78
  120.2 1.6 reshape.152
  121.8 1.9 fusion.6
  123.7 1.2 fusion.50
  124.9 6.7 %all-to-all-done.1 = bf16[128,2,128]{2,1,0:T(2,128)(2,1)} async-done(((bf16[128,2,128]{2,1,0:T(2,128)(2,1)}), bf16[128,2,128]{2,1,0:T(2,128)(2,1)}, u32[]{:S(2)}, u32[]{:S(2)}) %all-to-all-start.1) | async-done | bytes 65568 | tf_op jit(solution)/shard_map/all_to_all | solution.py:78
  132.6 2.1 fusion.7
  136.4 7.4 %all-to-all-start.5 = ((bf16[128,2,128]{2,1,0:T(2,128)(2,1)}), bf16[128,2,128]{2,1,0:T(2,128)(2,1)S(1)}, u32[]{:S(2)}, u32[]{:S(2)}) async-start(bf16[128,2,128]{2,1,0:T(2,128)(2,1)} %convert_element_type.92), calls=%async_computation.5 | async-start | bytes 131072 | tf_op jit(solution)/shard_map/all_to_all | solution.py:88
  143.8 2.7 fusion.18
  146.5 1.1 copy.69
  147.6 7.6 %all-to-all-done.5 = bf16[128,2,128]{2,1,0:T(2,128)(2,1)S(1)} async-done(((bf16[128,2,128]{2,1,0:T(2,128)(2,1)}), bf16[128,2,128]{2,1,0:T(2,128)(2,1)S(1)}, u32[]{:S(2)}, u32[]{:S(2)}) %all-to-all-start.5) | async-done | bytes 65568 | tf_op jit(solution)/shard_map/all_to_all | solution.py:88
  155.2 2.0 scatter_custom_fusion
  157.2 2.2 fusion.28
  159.4 3.3 %convolution_add_fusion = f32[512,512]{1,0:T(8,128)} fusion(f32[512,512]{1,0:T(8,128)} %fusion.28, bf16[512,512]{1,0:T(8,128)(2,1)} %param.24, bf16[512,512]{1,0:T(8,128)(2,1)S(1)} %fusion.11, bf16[512,512]{1,0:T(8,128)(2,1)} %param.23, f32[512,512]{1,0:T(8,128)S(1)} %fusion.55), kind=kOutput, calls=%fused_computation.12 | convolution fusion | flops 538705920 | bytes 4718592 | tf_op jit(solution)/shard_map/dot_general | solution.py:108
  165.3 18.2 %reduce-scatter.2.cloned.1.call-done = f32[128,512]{1,0:T(8,128)} async-done(((f32[512,512]{1,0:T(8,128)}), f32[128,512]{1,0:T(8,128)}) %reduce-scatter.2.cloned.1.call-update) | async-done | bytes 262160 | tf_op jit(solution)/shard_map/reduce_scatter | solution.py:107
  184.9 98.6 %psum.7 = f32[16,512]{1,0:T(8,128)S(1)} all-reduce(f32[16,512]{1,0:T(8,128)S(1)} %fusion.38), channel_id=1, replica_groups=mesh['round'=128,'mp'=4] {'round','mp'}, use_global_device_ids=true, to_apply=%region_8.9 | all-reduce | flops 8192 | bytes 65536 | tf_op jit(solution)/shard_map/psum | solution.py:123
  (60 shorter events, 17.2 us)
Async XLA Ops:
  7.2 20.7 %copy-start = (bf16[1,512,512]{2,1,0:T(8,128)(2,1)S(1)}, bf16[1,512,512]{2,1,0:T(8,128)(2,1)}, u32[]{:S(2)}) copy-start(bf16[1,512,512]{2,1,0:T(8,128)(2,1)} %param.13) | copy-start | bytes 1572868
  8.7 29.8 %all-to-all-start.2 = ((bf16[128,1,2]{2,1,0:T(2,128)(2,1)}), bf16[128,1,2]{2,1,0:T(2,128)(2,1)S(1)}, u32[]{:S(2)}, u32[]{:S(2)}) async-start(bf16[128,1,2]{2,1,0:T(2,128)(2,1)} %copy.61), calls=%async_computation.2 | async-start | bytes 131072 | tf_op jit(solution)/shard_map/all_to_all | solution.py:79
  35.0 14.9 %copy-start.6 = (s32[1,128,2]{1,2,0:T(2,128)S(1)}, s32[1,128,2]{1,2,0:T(2,128)}, u32[]{:S(2)}) copy-start(s32[1,128,2]{1,2,0:T(2,128)} %param.15) | copy-start | bytes 3076
  38.5 31.9 %all-to-all-start = ((bf16[128,2,1024]{2,1,0:T(2,128)(2,1)}), bf16[128,2,1024]{2,1,0:T(2,128)(2,1)S(1)}, u32[]{:S(2)}, u32[]{:S(2)}) async-start(bf16[128,2,1024]{2,1,0:T(2,128)(2,1)} %reshape.218), calls=%async_computation | async-start | bytes 1048576 | tf_op jit(solution)/shard_map/all_to_all | solution.py:56
  71.9 0.7 copy-start.7
  72.1 0.9 copy-start.3
  72.6 0.9 copy-start.4
  77.0 17.0 %all-to-all-start.3 = ((bf16[128,2,128]{2,1,0:T(2,128)(2,1)}), bf16[128,2,128]{2,1,0:T(2,128)(2,1)}, u32[]{:S(2)}, u32[]{:S(2)}) async-start(bf16[128,2,128]{2,1,0:T(2,128)(2,1)} %bitcast.12), calls=%async_computation.3 | async-start | bytes 131072 | tf_op jit(solution)/shard_map/all_to_all | solution.py:76
  83.3 1.5 copy-start.5
  94.1 19.2 %all-to-all-start.4 = ((bf16[128,2,128]{2,1,0:T(2,128)(2,1)}), bf16[128,2,128]{2,1,0:T(2,128)(2,1)}, u32[]{:S(2)}, u32[]{:S(2)}) async-start(bf16[128,2,128]{2,1,0:T(2,128)(2,1)} %bitcast.78), calls=%async_computation.4 | async-start | bytes 131072 | tf_op jit(solution)/shard_map/all_to_all | solution.py:77
  113.3 18.3 %all-to-all-start.1 = ((bf16[128,2,128]{2,1,0:T(2,128)(2,1)}), bf16[128,2,128]{2,1,0:T(2,128)(2,1)}, u32[]{:S(2)}, u32[]{:S(2)}) async-start(bf16[128,2,128]{2,1,0:T(2,128)(2,1)} %bitcast.76), calls=%async_computation.1 | async-start | bytes 131072 | tf_op jit(solution)/shard_map/all_to_all | solution.py:78
  136.4 18.8 %all-to-all-start.5 = ((bf16[128,2,128]{2,1,0:T(2,128)(2,1)}), bf16[128,2,128]{2,1,0:T(2,128)(2,1)S(1)}, u32[]{:S(2)}, u32[]{:S(2)}) async-start(bf16[128,2,128]{2,1,0:T(2,128)(2,1)} %convert_element_type.92), calls=%async_computation.5 | async-start | bytes 131072 | tf_op jit(solution)/shard_map/all_to_all | solution.py:88
  143.8 39.8 %reduce-scatter.2.cloned.1.call-start = ((), (), s32[]{:S(2)}) async-start(), calls=%async_computation.7 | async-start | bytes 1310720 | tf_op jit(solution)/shard_map/reduce_scatter | solution.py:107
  162.7 0.8 copy-start.2
  163.5 120.0 %copy-start.8 = (f32[512]{0:T(512)S(1)}, f32[512]{0:T(512)}, u32[]{:S(2)}) copy-start(f32[512]{0:T(512)} %param.25) | copy-start | bytes 6148
  184.6 99.6 %copy-start.1 = (bf16[32,4,512]{2,1,0:T(4,128)(2,1)}, bf16[32,4,512]{2,1,0:T(4,128)(2,1)S(1)}, u32[]{:S(2)}) copy-start(bf16[32,4,512]{2,1,0:T(4,128)(2,1)S(1)} %reshape.153) | copy-start | bytes 393220
Sparse Core Ops, SparseCore 0:
  162.9 20.6 reduce-scatter.1
where the time goes:
time: 292 us; the launch traced here: 291 us
  blocking collectives  98.6 us (34%)
  waiting for transfers between devices  68.8 us (24%)
  starting transfers between devices  58.4 us (20%)
  local copies, waits for them, and re-layouts  20.8 us (7%)
  matrix products  19.2 us (7%)
  between operations  14.4 us (5%)
  other arithmetic  10.9 us (4%)
    psum x1, blocking collectives, shards(): pooled = lax.psum(partial_sum, ('round', 'mp'))  98.6 us
    all_to_all x1, waiting for transfers between devices, shards(): lax.all_to_all(permuted, 'round', split_axis=1, concat_axis=0, tiled=True)  19.6 us
    all_to_all x1, starting transfers between devices, shards(): lax.all_to_all(live_slot.astype(jnp.bfloat16), 'round', split_axis=0, con...  18.4 us
    reduce_scatter x1, waiting for transfers between devices, shards(): lax.psum_scatter(attn_part + jnp.dot(hidden, w_down, preferred_element_ty...  18.2 us
    all_to_all x1, starting transfers between devices, shards(): lax.all_to_all(permuted, 'round', split_axis=1, concat_axis=0, tiled=True)  11.3 us
    all_to_all x1, waiting for transfers between devices, shards(): lax.all_to_all(keys_all[safe_rows], 'round', split_axis=0, concat_axis=0,...  8.46 us
    all_to_all x1, starting transfers between devices, shards(): lax.all_to_all(keys_all[safe_rows], 'round', split_axis=0, concat_axis=0,...  8.03 us
    all_to_all x1, waiting for transfers between devices, shards(): lax.all_to_all(seam_attn.reshape(round_count, -1, head_width), 'round', s...  7.59 us
  transfers between devices with their start and end apart: 7, of which 7 were waited for; matrix products, arithmetic and copies ran while one was open for 10% of the time, Pallas kernels for 0%

commit v1 on v0

--- a/solution.py
+++ b/solution.py
@@ -6,6 +6,11 @@
 
 HDIM = 64
 norm_eps = 1e-06
+
+
+def one_after_other(x, axis_one, axis_two):
+    partial = lax.psum(x, axis_one)
+    return lax.psum(partial, axis_two)
 
 
 def normalize(rows_in, norm_gain):
@@ -120,7 +125,7 @@
     )
     support_count = round_count * jnp.sum(obs_mask.astype(jnp.float32), axis=1)
     divisor = jnp.sqrt(support_count)
-    pooled = lax.psum(partial_sum, ("round", "mp"))
+    pooled = one_after_other(partial_sum, "round", "mp")
     obs_logits = jnp.dot(pooled, w_read, precision=lax.Precision.HIGHEST) / divisor
     return (tiles_out, obs_logits)
 

time: 292 us -> 703 us (2.41)
  blocking collectives: 98.6 us -> 503 us
    psum x1 -> x2, blocking collectives: 98.6 us -> 503 us  [the longest x1 492 us: one_after_other(): partial = lax.psum(x, axis_one)]
  transfers between devices with their start and end apart: 7 -> 7, of which waited for: 7 -> 7; matrix products, arithmetic and copies ran while one was open for 10% -> 4% of each run, Pallas kernels for 0% -> 0%
where the time goes in v1:
time: 703 us; the launch traced here: 696 us
  blocking collectives  503 us (72%)
  waiting for transfers between devices  68.8 us (10%)
  starting transfers between devices  58.4 us (8%)
  local copies, waits for them, and re-layouts  20.8 us (3%)
  matrix products  19.2 us (3%)
  between operations  14.4 us (2%)
  other arithmetic  10.9 us (2%)
    psum x1, blocking collectives, one_after_other(): partial = lax.psum(x, axis_one)  492 us
    all_to_all x1, waiting for transfers between devices, shards(): lax.all_to_all(permuted, 'round', split_axis=1, concat_axis=0, tiled=True)  19.6 us
    all_to_all x1, starting transfers between devices, shards(): lax.all_to_all(live_slot.astype(jnp.bfloat16), 'round', split_axis=0, con...  18.4 us
    reduce_scatter x1, waiting for transfers between devices, shards(): lax.psum_scatter(attn_part + jnp.dot(hidden, w_down, preferred_element_ty...  18.2 us
  transfers between devices with their start and end apart: 7, of which 7 were waited for; matrix products, arithmetic and copies ran while one was open for 4% of the time, Pallas kernels for 0%

profile of v1, /device:TPU:1, one launch (start us, length us, event | category | flops | bytes accessed | tf_op | source)
XLA Modules:
  0.0 695.7 jit_solution(7719618534248946246)
XLA Ops:
  8.7 18.4 %all-to-all-start.2 = ((bf16[128,1,2]{2,1,0:T(2,128)(2,1)}), bf16[128,1,2]{2,1,0:T(2,128)(2,1)S(1)}, u32[]{:S(2)}, u32[]{:S(2)}) async-start(bf16[128,1,2]{2,1,0:T(2,128)(2,1)} %copy.61), calls=%async_computation.2 | async-start | bytes 131072 | tf_op jit(solution)/shard_map/all_to_all | solution.py:84
  27.8 2.0 gather_fusion
  31.1 3.8 reduce.2
  35.0 1.1 reshape.218
  36.1 2.4 all-to-all-done.2
  38.5 11.3 %all-to-all-start = ((bf16[128,2,1024]{2,1,0:T(2,128)(2,1)}), bf16[128,2,1024]{2,1,0:T(2,128)(2,1)S(1)}, u32[]{:S(2)}, u32[]{:S(2)}) async-start(bf16[128,2,1024]{2,1,0:T(2,128)(2,1)} %reshape.218), calls=%async_computation | async-start | bytes 1048576 | tf_op jit(solution)/shard_map/all_to_all | solution.py:61
  50.8 19.6 %all-to-all-done = bf16[128,2,1024]{2,1,0:T(2,128)(2,1)S(1)} async-done(((bf16[128,2,1024]{2,1,0:T(2,128)(2,1)}), bf16[128,2,1024]{2,1,0:T(2,128)(2,1)S(1)}, u32[]{:S(2)}, u32[]{:S(2)}) %all-to-all-start) | async-done | bytes 524320 | tf_op jit(solution)/shard_map/all_to_all | solution.py:61
  70.9 1.1 bitcast_convert_fusion
  74.1 1.5 gather_fusion.1
  75.6 1.5 gather_fusion.2
  77.0 6.3 all-to-all-start.3
  83.3 1.5 fusion.55
  86.8 1.5 gather_fusion.3
  88.3 5.8 all-to-all-done.3
  94.1 8.0 %all-to-all-start.4 = ((bf16[128,2,128]{2,1,0:T(2,128)(2,1)}), bf16[128,2,128]{2,1,0:T(2,128)(2,1)}, u32[]{:S(2)}, u32[]{:S(2)}) async-start(bf16[128,2,128]{2,1,0:T(2,128)(2,1)} %bitcast.78), calls=%async_computation.4 | async-start | bytes 131072 | tf_op jit(solution)/shard_map/all_to_all | solution.py:82
  102.1 1.7 fusion.49
  104.8 8.5 %all-to-all-done.4 = bf16[128,2,128]{2,1,0:T(2,128)(2,1)} async-done(((bf16[128,2,128]{2,1,0:T(2,128)(2,1)}), bf16[128,2,128]{2,1,0:T(2,128)(2,1)}, u32[]{:S(2)}, u32[]{:S(2)}) %all-to-all-start.4) | async-done | bytes 65568 | tf_op jit(solution)/shard_map/all_to_all | solution.py:82
  113.3 6.9 all-to-all-start.1
  120.2 1.6 reshape.152
  121.8 1.9 fusion.6
  123.7 1.2 fusion.50
  124.9 6.7 all-to-all-done.1
  132.6 2.1 fusion.7
  136.4 7.4 %all-to-all-start.5 = ((bf16[128,2,128]{2,1,0:T(2,128)(2,1)}), bf16[128,2,128]{2,1,0:T(2,128)(2,1)S(1)}, u32[]{:S(2)}, u32[]{:S(2)}) async-start(bf16[128,2,128]{2,1,0:T(2,128)(2,1)} %convert_element_type.92), calls=%async_computation.5 | async-start | bytes 131072 | tf_op jit(solution)/shard_map/all_to_all | solution.py:93
  143.8 2.7 fusion.18
  147.6 7.6 %all-to-all-done.5 = bf16[128,2,128]{2,1,0:T(2,128)(2,1)S(1)} async-done(((bf16[128,2,128]{2,1,0:T(2,128)(2,1)}), bf16[128,2,128]{2,1,0:T(2,128)(2,1)S(1)}, u32[]{:S(2)}, u32[]{:S(2)}) %all-to-all-start.5) | async-done | bytes 65568 | tf_op jit(solution)/shard_map/all_to_all | solution.py:93
  155.2 2.0 scatter_custom_fusion
  157.2 2.2 fusion.28
  159.4 3.3 convolution_add_fusion
  165.3 18.2 %reduce-scatter.2.cloned.1.call-done = f32[128,512]{1,0:T(8,128)} async-done(((f32[512,512]{1,0:T(8,128)}), f32[128,512]{1,0:T(8,128)}) %reduce-scatter.2.cloned.1.call-update) | async-done | bytes 262160 | tf_op jit(solution)/shard_map/reduce_scatter | solution.py:112
  184.9 491.7 %psum.14 = f32[16,512]{1,0:T(8,128)S(1)} all-reduce(f32[16,512]{1,0:T(8,128)S(1)} %fusion.38), channel_id=1, replica_groups=mesh['round'=128,'mp'=4] {'round'}, use_global_device_ids=true, to_apply=%region_8.9 | all-reduce | flops 8192 | bytes 65536 | tf_op jit(solution)/shard_map/psum | solution.py:12
  676.6 11.5 %psum.15 = f32[16,512]{1,0:T(8,128)S(1)} all-reduce(f32[16,512]{1,0:T(8,128)S(1)} %psum.14), channel_id=1, replica_groups=mesh['round'=128,'mp'=4] {'mp'}, use_global_device_ids=true, to_apply=%region_9.10 | all-reduce | flops 8192 | bytes 65536 | tf_op jit(solution)/shard_map/psum | solution.py:13
  (61 shorter events, 18.2 us)
Async XLA Ops:
  7.2 20.7 %copy-start = (bf16[1,512,512]{2,1,0:T(8,128)(2,1)S(1)}, bf16[1,512,512]{2,1,0:T(8,128)(2,1)}, u32[]{:S(2)}) copy-start(bf16[1,512,512]{2,1,0:T(8,128)(2,1)} %param.13) | copy-start | bytes 1572868
  8.7 29.8 %all-to-all-start.2 = ((bf16[128,1,2]{2,1,0:T(2,128)(2,1)}), bf16[128,1,2]{2,1,0:T(2,128)(2,1)S(1)}, u32[]{:S(2)}, u32[]{:S(2)}) async-start(bf16[128,1,2]{2,1,0:T(2,128)(2,1)} %copy.61), calls=%async_computation.2 | async-start | bytes 131072 | tf_op jit(solution)/shard_map/all_to_all | solution.py:84
  35.0 14.9 %copy-start.6 = (s32[1,128,2]{1,2,0:T(2,128)S(1)}, s32[1,128,2]{1,2,0:T(2,128)}, u32[]{:S(2)}) copy-start(s32[1,128,2]{1,2,0:T(2,128)} %param.15) | copy-start | bytes 3076
  38.5 31.9 %all-to-all-start = ((bf16[128,2,1024]{2,1,0:T(2,128)(2,1)}), bf16[128,2,1024]{2,1,0:T(2,128)(2,1)S(1)}, u32[]{:S(2)}, u32[]{:S(2)}) async-start(bf16[128,2,1024]{2,1,0:T(2,128)(2,1)} %reshape.218), calls=%async_computation | async-start | bytes 1048576 | tf_op jit(solution)/shard_map/all_to_all | solution.py:61
  71.9 0.7 copy-start.7
  72.1 0.9 copy-start.3
  72.6 0.9 copy-start.4
  77.0 17.0 %all-to-all-start.3 = ((bf16[128,2,128]{2,1,0:T(2,128)(2,1)}), bf16[128,2,128]{2,1,0:T(2,128)(2,1)}, u32[]{:S(2)}, u32[]{:S(2)}) async-start(bf16[128,2,128]{2,1,0:T(2,128)(2,1)} %bitcast.12), calls=%async_computation.3 | async-start | bytes 131072 | tf_op jit(solution)/shard_map/all_to_all | solution.py:81
  83.3 1.5 copy-start.5
  94.1 19.2 %all-to-all-start.4 = ((bf16[128,2,128]{2,1,0:T(2,128)(2,1)}), bf16[128,2,128]{2,1,0:T(2,128)(2,1)}, u32[]{:S(2)}, u32[]{:S(2)}) async-start(bf16[128,2,128]{2,1,0:T(2,128)(2,1)} %bitcast.78), calls=%async_computation.4 | async-start | bytes 131072 | tf_op jit(solution)/shard_map/all_to_all | solution.py:82
  113.3 18.3 %all-to-all-start.1 = ((bf16[128,2,128]{2,1,0:T(2,128)(2,1)}), bf16[128,2,128]{2,1,0:T(2,128)(2,1)}, u32[]{:S(2)}, u32[]{:S(2)}) async-start(bf16[128,2,128]{2,1,0:T(2,128)(2,1)} %bitcast.76), calls=%async_computation.1 | async-start | bytes 131072 | tf_op jit(solution)/shard_map/all_to_all | solution.py:83
  136.4 18.8 %all-to-all-start.5 = ((bf16[128,2,128]{2,1,0:T(2,128)(2,1)}), bf16[128,2,128]{2,1,0:T(2,128)(2,1)S(1)}, u32[]{:S(2)}, u32[]{:S(2)}) async-start(bf16[128,2,128]{2,1,0:T(2,128)(2,1)} %convert_element_type.92), calls=%async_computation.5 | async-start | bytes 131072 | tf_op jit(solution)/shard_map/all_to_all | solution.py:93
  143.8 39.8 %reduce-scatter.2.cloned.1.call-start = ((), (), s32[]{:S(2)}) async-start(), calls=%async_computation.7 | async-start | bytes 1310720 | tf_op jit(solution)/shard_map/reduce_scatter | solution.py:112
  162.7 0.8 copy-start.2
  163.5 524.7 %copy-start.8 = (f32[512]{0:T(512)S(1)}, f32[512]{0:T(512)}, u32[]{:S(2)}) copy-start(f32[512]{0:T(512)} %param.25) | copy-start | bytes 6148
  184.6 504.3 %copy-start.1 = (bf16[32,4,512]{2,1,0:T(4,128)(2,1)}, bf16[32,4,512]{2,1,0:T(4,128)(2,1)S(1)}, u32[]{:S(2)}) copy-start(bf16[32,4,512]{2,1,0:T(4,128)(2,1)S(1)} %reshape.153) | copy-start | bytes 393220
Sparse Core Ops, SparseCore 0:
  162.9 20.6 reduce-scatter.1
